TPU v7x, 128 devices: a whole 4x4x4 slice. The times are simulated.
128 devices in a mesh: row: 8 (over z_lo, y), col: 16 (over z_hi, x, core).
Axes of the slice: x: 4, y: 4, z: 4 (z_hi: 2, z_lo: 2; z = z_hi * 2 + z_lo), core: 2. Of those that a mesh axis runs over, the one named last changes fastest.
Arguments:
- density: float32 [6144, 6144], P('row', 'col'), may hold values from -1 to 1, as said below
- response: float32 [6144, 6144], P('row', 'col'), may hold values from -1 to 1, as said below
- density_mask: int32 [48, 48], replicated, may hold values from 0 to 1, as said below
- response_mask: int32 [48, 48], replicated, may hold values from 0 to 1, as said below
- branch: int32 [48], replicated, may hold values from 0 to 1
Outputs:
- new_density: float32 [6144, 6144], P('row', 'col')
- new_response: float32 [6144, 6144], P('row', 'col')
Inputs may be any that keep to these rules, and one draw needn't show every extreme that they name: `density`: symmetric: equal to its own transpose. `response`: symmetric: equal to its own transpose. `density_mask`: symmetric, with ones on the diagonal. `response_mask`: symmetric, with ones on the diagonal.
All inputs are finite; a program needn't handle non-finite values.
Results may differ from a plain program's by a relative error of at most 0.000067.
Values sent between devices are 32-bit elements; how exact they have to be, the bound alone decides.
No kernel may reach another device: no remote copies, remote signals or barrier semaphores. Data moves between devices by JAX's collectives and lax.ppermute only.
A program may use at most 192 MiB of HBM per device.

v0:
```python
import jax
import jax.numpy as jnp
from jax import lax
from jax.sharding import PartitionSpec as P

BLOCK = 128
precise = lax.Precision.HIGHEST


def in_one_piece(arrays, axis, dim, along):
    ends, at = ([], 0)
    for a in arrays[:-1]:
        at += a.shape[along]
        ends.append(at)
    both = jnp.concatenate(arrays, axis=along)
    return tuple(jnp.split(lax.all_gather(both, axis, axis=dim, tiled=True), ends, axis=along))


def expand_mask(local_tile, block_mask):
    row_count, col_count = local_tile.shape
    row_blocks = row_count // BLOCK
    col_blocks = col_count // BLOCK
    row_start = lax.axis_index("row") * row_blocks
    col_start = lax.axis_index("col") * col_blocks
    window = lax.dynamic_slice(block_mask, (row_start, col_start), (row_blocks, col_blocks)).astype(
        jnp.float32
    )
    shaped = local_tile.reshape(row_blocks, BLOCK, col_blocks, BLOCK) * window[:, None, :, None]
    return shaped.reshape(row_count, col_count)


def matmul(left, right):
    return jnp.dot(left, right, precision=precise, preferred_element_type=jnp.float32)


def per_device(density, response, density_mask, response_mask, branch):
    masked_density = expand_mask(density, density_mask)
    masked_response = expand_mask(response, response_mask)
    column_density, column_response = (
        lax.all_gather(masked_density, "row", axis=0, tiled=True),
        lax.all_gather(masked_response, "row", axis=0, tiled=True),
    )
    segments = in_one_piece((masked_density, masked_response), "col", 1, 0)
    square = matmul(segments[0], column_density)
    product = matmul(segments[0], column_response)
    reversed_tile = matmul(segments[1], column_density)
    combined = product + reversed_tile
    local_blocks = density.shape[0] // BLOCK
    block_start = lax.axis_index("row") * local_blocks
    local_branch = lax.dynamic_slice_in_dim(branch, block_start, local_blocks, 0)
    chosen = jnp.repeat(local_branch, BLOCK)[:, None]
    new_density = jnp.where(chosen == 0, square, 2.0 * masked_density - square)
    new_response = jnp.where(chosen == 0, combined, 2.0 * masked_response - combined)
    return (new_density, new_response)


def solution(mesh):
    return jax.shard_map(
        per_device,
        mesh=mesh,
        in_specs=(P("row", "col"), P("row", "col"), P(), P(), P()),
        out_specs=(P("row", "col"), P("row", "col")),
        check_vma=False,
    )
```

profile of v0, /device:TPU:1, one launch (start us, length us, event | category | flops | bytes accessed | tf_op | source)
XLA Modules:
  0.0 463.0 jit_solution(11147713963077403689)
XLA Ops:
  7.2 0.0 all-gather.6.cloned.1.call-start
  7.2 0.8 dynamic-slice_convert_fusion
  8.0 0.1 copy.7
  8.1 0.2 mul.39
  8.3 0.3 copy.16
  8.6 0.0 copy-start.4
  8.6 0.4 copy.8
  8.9 0.9 copy-done.4
  9.8 1.1 mul.41
  11.0 0.0 all-gather.6.cloned.1.call-update
  11.0 0.0 all-gather.4.cloned.1.call-start
  11.0 0.1 copy.9
  11.1 0.2 mul.42
  11.3 0.3 copy.15
  11.6 0.4 copy.10
  11.9 0.0 copy-start.1
  11.9 1.5 mul.44
  13.4 0.0 copy-start.2
  13.4 0.1 copy-done.1
  13.6 1.7 pad_maximum_fusion
  15.2 0.0 copy-done.2
  15.2 0.0 copy-start.5
  15.3 0.0 all-gather.4.cloned.1.call-update
  15.3 0.0 all-gather.8.cloned.1.call-start
  15.3 0.7 all-gather.8.cloned.1.call-update
  16.0 0.0 copy-done.5
  16.0 0.1 dynamic-slice_compare_fusion
  16.1 0.1 broadcast_bitcast_fusion
  16.2 99.8 %all-gather.6.cloned.1.call-done = f32[6144,384]{1,0:T(8,128)} async-done(((f32[768,384]{1,0:T(8,128)}), f32[6144,384]{1,0:T(8,128)}) %all-gather.6.cloned.1.call-update) | async-done | bytes 9437200 | tf_op jit(solution)/shard_map/all_gather | solution.py:40
  115.9 205.9 %all-gather.4.cloned.1.call-done = f32[1536,6144]{1,0:T(8,128)} async-done(((f32[1536,384]{1,0:T(8,128)}), f32[1536,6144]{1,0:T(8,128)}) %all-gather.4.cloned.1.call-update) | async-done | bytes 37748752 | tf_op jit(solution)/shard_map/all_gather | solution.py:16
  321.9 0.0 copy-start
  321.9 34.6 %fusion = f32[768,384]{1,0:T(8,128)S(1)} fusion(f32[6144,384]{1,0:T(8,128)} %all-gather.6.cloned.1.call-done, f32[1536,6144]{1,0:T(8,128)} %all-gather.4.cloned.1.call-done), kind=kOutput, calls=%fused_computation | convolution fusion | flops 21743271936 | bytes 29491200 | tf_op jit(solution)/shard_map/dot_general | solution.py:33
  356.5 0.0 copy-done
  356.5 0.0 copy-start.3
  356.5 41.1 %subtract_select_fusion.1 = f32[768,384]{1,0:T(8,128)} fusion(f32[6144,384]{1,0:T(8,128)S(1)} %copy-done, f32[1536,6144]{1,0:T(8,128)} %all-gather.4.cloned.1.call-done, f32[768,384]{1,0:T(8,128)S(1)} %copy-done.1, pred[768]{0:T(1024)(128)(4,1)S(1)} %broadcast_bitcast_fusion), kind=kOutput, calls=%fused_computation.8 | convolution fusion | flops 21744156672 | bytes 30671616 | tf_op jit(solution)/shard_map/dot_general | solution.py:33
  397.6 24.5 %all-gather.8.cloned.1.call-done = f32[6144,384]{1,0:T(8,128)} async-done(((f32[768,384]{1,0:T(8,128)}), f32[6144,384]{1,0:T(8,128)}) %all-gather.8.cloned.1.call-update) | async-done | bytes 9437200 | tf_op jit(solution)/shard_map/all_gather | solution.py:41
  422.2 0.0 copy-done.3
  422.2 34.3 %subtract_select_fusion = f32[768,384]{1,0:T(8,128)} fusion(f32[768,384]{1,0:T(8,128)S(1)} %fusion, f32[6144,384]{1,0:T(8,128)} %all-gather.8.cloned.1.call-done, f32[1536,6144]{1,0:T(8,128)} %all-gather.4.cloned.1.call-done, f32[768,384]{1,0:T(8,128)S(1)} %copy-done.3, pred[768]{0:T(1024)(128)(4,1)S(1)} %broadcast_bitcast_fusion), kind=kOutput, calls=%fused_computation.7 | convolution fusion | flops 21744451584 | bytes 31851264 | tf_op jit(solution)/shard_map/dot_general | solution.py:33
Async XLA Ops:
  7.2 108.8 %all-gather.6.cloned.1.call-start = ((), (), s32[]{:S(2)}) async-start(), calls=%async_computation.1 | async-start | bytes 10616832 | tf_op jit(solution)/shard_map/all_gather | solution.py:40
  8.6 1.3 copy-start.4
  11.0 310.9 %all-gather.4.cloned.1.call-start = ((), (), s32[]{:S(2)}) async-start(), calls=%async_computation | async-start | bytes 40108032 | tf_op jit(solution)/shard_map/all_gather | solution.py:16
  11.9 1.6 copy-start.1
  13.4 1.8 copy-start.2
  15.2 0.8 copy-start.5
  15.3 406.9 %all-gather.8.cloned.1.call-start = ((), (), s32[]{:S(2)}) async-start(), calls=%async_computation.2 | async-start | bytes 10616832 | tf_op jit(solution)/shard_map/all_gather | solution.py:41
  321.9 34.6 %copy-start = (f32[6144,384]{1,0:T(8,128)S(1)}, f32[6144,384]{1,0:T(8,128)}, u32[]{:S(2)}) copy-start(f32[6144,384]{1,0:T(8,128)} %all-gather.6.cloned.1.call-done) | copy-start | bytes 28311556
  356.5 65.7 %copy-start.3 = (f32[768,384]{1,0:T(8,128)S(1)}, f32[768,384]{1,0:T(8,128)}, u32[]{:S(2)}) copy-start(f32[768,384]{1,0:T(8,128)} %copy-done.2) | copy-start | bytes 3538948
Sparse Core Ops, SparseCore 0:
  11.1 104.7 all-gather.5
  118.4 203.4 all-gather.3
  323.5 98.6 all-gather.7
where the time goes:
time: 463 us
  waiting for transfers between devices  331 us (71%)
  matrix products  110 us (24%)
  between operations  13.9 us (3%)
  other arithmetic  5.18 us (1%)
    all_gather x1, waiting for transfers between devices, in_one_piece(): lax.all_gather(both, axis, axis=dim, tiled=True)  206 us
    dot_general x3, matrix products, matmul(): jnp.dot(left, right, precision=precise, preferred_element_type=jnp.float32)  110 us
    all_gather x1, waiting for transfers between devices, per_device(): lax.all_gather(masked_density, 'row', axis=0, tiled=True)  99.8 us
    all_gather x1, waiting for transfers between devices, per_device(): lax.all_gather(masked_response, 'row', axis=0, tiled=True)  24.5 us
  transfers between devices with their start and end apart: 3, of which 3 were waited for; matrix products, arithmetic and copies ran while one was open for 17% of the time, Pallas kernels for 0%

commit v1 on v0

--- a/solution.py
+++ b/solution.py
@@ -37,7 +37,9 @@
     masked_density = expand_mask(density, density_mask)
     masked_response = expand_mask(response, response_mask)
     column_density, column_response = (
-        lax.all_gather(masked_density, "row", axis=0, tiled=True),
+        jnp.concatenate(
+            lax.all_to_all(jnp.stack([masked_density] * lax.axis_size("row")), "row", 0, 0), axis=0
+        ),
         lax.all_gather(masked_response, "row", axis=0, tiled=True),
     )
     segments = in_one_piece((masked_density, masked_response), "col", 1, 0)

time: 463 us -> 461 us (level)
  matrix products: 110 us -> 102 us
  starting transfers between devices: 0.12 us -> 6.57 us
    all_to_all x0 -> x1, waiting for transfers between devices: none -> 122 us  [per_device(): lax.all_to_all(jnp.stack([masked_density] * lax.axis_size('row')), 'row',...]
    all_gather x1 -> x0, waiting for transfers between devices: 99.8 us -> none  [per_device(): lax.all_gather(masked_density, 'row', axis=0, tiled=True)]
    all_gather x1, waiting for transfers between devices: 206 us -> 172 us  [in_one_piece(): lax.all_gather(both, axis, axis=dim, tiled=True)]
    all_gather x1, waiting for transfers between devices: 24.5 us -> 33.3 us  [per_device(): lax.all_gather(masked_response, 'row', axis=0, tiled=True)]
    dot_general x3, matrix products: 110 us -> 102 us  [matmul(): jnp.dot(left, right, precision=precise, preferred_element_type=jnp.float32)]
    all_to_all x0 -> x1, starting transfers between devices: none -> 6.5 us  [per_device(): lax.all_to_all(jnp.stack([masked_density] * lax.axis_size('row')), 'row',...]
  transfers between devices with their start and end apart: 3 -> 3, of which waited for: 3 -> 3; matrix products, arithmetic and copies ran while one was open for 17% -> 16% of each run, Pallas kernels for 0% -> 0%
where the time goes in v1:
time: 461 us
  waiting for transfers between devices  328 us (71%)
  matrix products  102 us (22%)
  between operations  14.1 us (3%)
  starting transfers between devices  6.57 us (1%)
  local copies, waits for them, and re-layouts  6.22 us (1%)
    all_gather x1, waiting for transfers between devices, in_one_piece(): lax.all_gather(both, axis, axis=dim, tiled=True)  172 us
    all_to_all x1, waiting for transfers between devices, per_device(): lax.all_to_all(jnp.stack([masked_density] * lax.axis_size('row')), 'row',...  122 us
    dot_general x3, matrix products, matmul(): jnp.dot(left, right, precision=precise, preferred_element_type=jnp.float32)  102 us
    all_gather x1, waiting for transfers between devices, per_device(): lax.all_gather(masked_response, 'row', axis=0, tiled=True)  33.3 us
  transfers between devices with their start and end apart: 3, of which 3 were waited for; matrix products, arithmetic and copies ran while one was open for 16% of the time, Pallas kernels for 0%

profile of v1, /device:TPU:1, one launch (start us, length us, event | category | flops | bytes accessed | tf_op | source)
XLA Modules:
  0.0 460.8 jit_solution(14790313708173095497)
XLA Ops:
  7.2 0.0 all-gather.3.cloned.1.call-start
  7.2 0.8 dynamic-slice_convert_fusion
  8.0 0.1 copy.7
  8.1 0.2 mul.41
  8.3 0.3 copy.16
  8.6 0.4 copy.8
  8.9 0.1 copy.9
  9.0 0.2 mul.44
  9.2 0.3 copy.15
  9.5 0.4 copy.10
  9.8 0.0 copy-start.2
  9.8 1.5 mul.43
  11.3 0.1 copy-done.2
  11.5 0.1 mul.46
  11.6 0.0 copy-start
  11.6 1.7 pad_maximum_fusion
  13.3 0.0 copy-done
  13.4 0.0 all-gather.3.cloned.1.call-update
  13.4 0.0 all-gather.5.cloned.1.call-start
  13.4 0.7 all-gather.5.cloned.1.call-update
  14.1 4.2 stack.3
  18.3 0.0 copy-start.3
  18.3 6.5 %all-to-all-start = ((f32[8,768,384]{2,1,0:T(8,128)}), f32[8,768,384]{2,1,0:T(8,128)}, u32[]{:S(2)}, u32[]{:S(2)}) async-start(f32[8,768,384]{2,1,0:T(8,128)} %stack.3), calls=%async_computation | async-start | bytes 18874368 | tf_op jit(solution)/shard_map/all_to_all | solution.py:41
  24.8 0.0 copy-done.3
  24.8 0.1 dynamic-slice_compare_fusion
  24.9 0.1 broadcast_bitcast_fusion
  25.0 122.0 %all-to-all-done = f32[8,768,384]{2,1,0:T(8,128)} async-done(((f32[8,768,384]{2,1,0:T(8,128)}), f32[8,768,384]{2,1,0:T(8,128)}, u32[]{:S(2)}, u32[]{:S(2)}) %all-to-all-start) | async-done | bytes 9437216 | tf_op jit(solution)/shard_map/all_to_all | solution.py:41
  147.0 171.7 %all-gather.3.cloned.1.call-done = f32[1536,6144]{1,0:T(8,128)} async-done(((f32[1536,384]{1,0:T(8,128)}), f32[1536,6144]{1,0:T(8,128)}) %all-gather.3.cloned.1.call-update) | async-done | bytes 37748752 | tf_op jit(solution)/shard_map/all_gather | solution.py:16
  318.7 33.1 %fusion = f32[768,384]{1,0:T(8,128)S(1)} fusion(f32[6144,384]{1,0:T(8,128)} %bitcast.1, f32[1536,6144]{1,0:T(8,128)} %all-gather.3.cloned.1.call-done), kind=kOutput, calls=%fused_computation | convolution fusion | flops 21743271936 | bytes 29491200 | tf_op jit(solution)/shard_map/dot_general | solution.py:33
  351.8 0.0 copy-start.1
  351.8 34.5 %subtract_select_fusion.1 = f32[768,384]{1,0:T(8,128)} fusion(f32[6144,384]{1,0:T(8,128)} %bitcast.1, f32[1536,6144]{1,0:T(8,128)} %all-gather.3.cloned.1.call-done, f32[768,384]{1,0:T(8,128)S(1)} %mul.43, pred[768]{0:T(1024)(128)(4,1)S(1)} %broadcast_bitcast_fusion), kind=kOutput, calls=%fused_computation.8 | convolution fusion | flops 21744156672 | bytes 30671616 | tf_op jit(solution)/shard_map/dot_general | solution.py:33
  386.3 33.3 %all-gather.5.cloned.1.call-done = f32[6144,384]{1,0:T(8,128)} async-done(((f32[768,384]{1,0:T(8,128)}), f32[6144,384]{1,0:T(8,128)}) %all-gather.5.cloned.1.call-update) | async-done | bytes 9437200 | tf_op jit(solution)/shard_map/all_gather | solution.py:43
  419.6 0.0 copy-done.1
  419.6 34.3 %subtract_select_fusion = f32[768,384]{1,0:T(8,128)} fusion(f32[768,384]{1,0:T(8,128)S(1)} %fusion, f32[6144,384]{1,0:T(8,128)} %all-gather.5.cloned.1.call-done, f32[1536,6144]{1,0:T(8,128)} %all-gather.3.cloned.1.call-done, f32[768,384]{1,0:T(8,128)S(1)} %copy-done.1, pred[768]{0:T(1024)(128)(4,1)S(1)} %broadcast_bitcast_fusion), kind=kOutput, calls=%fused_computation.7 | convolution fusion | flops 21744451584 | bytes 31851264 | tf_op jit(solution)/shard_map/dot_general | solution.py:33
Async XLA Ops:
  7.2 311.6 %all-gather.3.cloned.1.call-start = ((), (), s32[]{:S(2)}) async-start(), calls=%async_computation.1 | async-start | bytes 40108032 | tf_op jit(solution)/shard_map/all_gather | solution.py:16
  9.8 1.6 copy-start.2
  11.6 1.8 copy-start
  13.4 406.2 %all-gather.5.cloned.1.call-start = ((), (), s32[]{:S(2)}) async-start(), calls=%async_computation.2 | async-start | bytes 10616832 | tf_op jit(solution)/shard_map/all_gather | solution.py:43
  18.3 6.5 %copy-start.3 = (s32[48]{0:T(128)S(1)}, s32[48]{0:T(128)}, u32[]{:S(2)}) copy-start(s32[48]{0:T(128)} %param.9) | copy-start | bytes 580
  18.3 128.7 %all-to-all-start = ((f32[8,768,384]{2,1,0:T(8,128)}), f32[8,768,384]{2,1,0:T(8,128)}, u32[]{:S(2)}, u32[]{:S(2)}) async-start(f32[8,768,384]{2,1,0:T(8,128)} %stack.3), calls=%async_computation | async-start | bytes 18874368 | tf_op jit(solution)/shard_map/all_to_all | solution.py:41
  351.8 67.8 %copy-start.1 = (f32[768,384]{1,0:T(8,128)S(1)}, f32[768,384]{1,0:T(8,128)}, u32[]{:S(2)}) copy-start(f32[768,384]{1,0:T(8,128)} %copy-done) | copy-start | bytes 3538948
Sparse Core Ops, SparseCore 0:
  13.5 305.1 all-gather.2
  320.9 98.6 all-gather.4
